TPU v7x, 32 devices: a whole 2x2x4 slice. The times are simulated.
32 devices in a mesh: tile: 8 (over z, y), depth: 4 (over x, core).
Axes of the slice: x: 2, y: 2, z: 4, core: 2. Of those that a mesh axis runs over, the one named last changes fastest.
Arguments:
- positions: float32 [3, 16384], P(None, 'tile'), may hold values from -4 to 4
- log_scales: float32 [3, 16384], P(None, 'tile'), may hold values from -2 to 0
- opacity_logits: float32 [1, 16384], P(None, 'tile'), may hold values from -3 to 1.5
- colors: float32 [3, 16384], P(None, 'tile'), may hold values from 0 to 1
- first_moment: float32 [10, 16384], P(None, 'tile'), may hold values from -3 to 3
- second_moment: float32 [10, 16384], P(None, 'tile'), may hold values from 0.01 to 1
- cameras: float32 [4, 2, 4], replicated, may hold values from -6.4 to 6.4
- background: float32 [3], replicated, may hold values from 0 to 1
- target: float32 [32, 3, 1024], P('tile'), may hold values from 0 to 1
- tile_view: int32 [32], P('tile'), may hold values from 0 to 3
- tile_length: int32 [32], P('tile'), may hold values from 128 to 512
- list_owner: int32 [4, 32, 128, 1], P('depth', 'tile'), may hold values from 0 to 7; in each aligned block of 512 rows (0 to 511, 512 to 1023, ..., all dimensions but the last counted through in order) at most 160 rows name the same one
- list_row: int32 [4, 32, 128], P('depth', 'tile'), may hold values from 0 to 2047
Outputs:
- image: float32 [32, 3, 1024], P('tile')
- new_params: float32 [10, 16384], P(None, 'tile')
- new_first: float32 [10, 16384], P(None, 'tile')
- new_second: float32 [10, 16384], P(None, 'tile')
Inputs may be any that keep to these rules, and one draw needn't show every extreme that they name: `list_owner`: within the entries of one device's block (one depth slab of the tiles of one tile index), no owner is named more than 160 times, a bound that some block reaches.
All inputs are finite; a program needn't handle non-finite values.
Results may differ from a plain program's by a relative error of at most 0.00008.
Values sent between devices are 32-bit elements; how exact they have to be, the bound alone decides.
A program may use at most 64 MiB of HBM per device.

v0:
```python
import jax
import jax.numpy as jnp
from jax import lax
from jax.sharding import PartitionSpec as P

TILE_SIDE = 32


def project(params, cams):
    position = params[0:3]
    variance = jnp.exp(2.0 * params[3:6])
    first_row = cams[:, 0, 0:3].T
    second_row = cams[:, 1, 0:3].T
    center_x = jnp.sum(first_row * position, axis=0) + cams[:, 0, 3] + 0.5 * TILE_SIDE
    center_y = jnp.sum(second_row * position, axis=0) + cams[:, 1, 3] + 0.5 * TILE_SIDE
    cov_xx = jnp.sum(first_row * first_row * variance, axis=0) + 0.3
    cov_xy = jnp.sum(first_row * second_row * variance, axis=0)
    cov_yy = jnp.sum(second_row * second_row * variance, axis=0) + 0.3
    determinant = cov_xx * cov_yy - cov_xy * cov_xy
    return jnp.stack(
        [
            center_x,
            center_y,
            cov_yy / determinant,
            -cov_xy / determinant,
            cov_xx / determinant,
            jax.nn.sigmoid(params[6]),
            params[7],
            params[8],
            params[9],
        ]
    )


def coverage(screen, alive, pixels):
    pixel = jnp.arange(pixels, dtype=jnp.int32)
    pixel_x = (pixel % TILE_SIDE).astype(jnp.float32) + 0.5
    pixel_y = (pixel // TILE_SIDE).astype(jnp.float32) + 0.5
    offset_x = pixel_x[:, None] - screen[0][None, :]
    offset_y = pixel_y[:, None] - screen[1][None, :]
    quadric = (
        screen[2][None, :] * offset_x * offset_x
        + 2.0 * screen[3][None, :] * offset_x * offset_y
        + screen[4][None, :] * offset_y * offset_y
    )
    falloff = jnp.exp(-0.5 * quadric)
    alpha = screen[5][None, :] * falloff * alive[None, :]
    return (offset_x, offset_y, falloff, alpha)


def running_sum(values, triangle):
    rows = values.shape[0]
    width = triangle.shape[0]
    blocks = values.reshape(rows, values.shape[1] // width, width)
    inner = jnp.einsum("pbk,kj->pbj", blocks, triangle, precision=lax.Precision.HIGHEST)
    sums = jnp.sum(blocks, axis=2)
    lead = jnp.cumsum(sums, axis=1) - sums
    return (inner + lead[:, :, None]).reshape(rows, values.shape[1])


def adam_update(param, first, second, gradient):
    new_first = 0.9 * first + 0.1 * gradient
    new_second = 0.999 * second + 0.001 * gradient * gradient
    corrected = new_first / (1.0 - 0.9**10) / (jnp.sqrt(new_second / (1.0 - 0.999**10)) + 1e-08)
    return (param - 0.05 * corrected, new_first, new_second)


def body(
    positions,
    log_scales,
    opacity_logits,
    colors,
    first_moment,
    second_moment,
    cameras,
    background,
    target,
    tile_view,
    tile_length,
    list_owner,
    list_row,
):
    tiles_here = target.shape[0]
    pixels = target.shape[2]
    slab = list_row.shape[2]
    owner_count = lax.axis_size("tile")
    depth_count = lax.axis_size("depth")
    depth_index = lax.axis_index("depth")
    capacity = max(2, 5 * tiles_here * slab // (2 * owner_count))
    highest = lax.Precision.HIGHEST
    params = jnp.concatenate([positions, log_scales, opacity_logits, colors], axis=0)
    owner = list_owner.reshape(-1)
    wanted = list_row.reshape(-1)
    viewed = jnp.repeat(tile_view, slab)
    onehot = (owner[:, None] == jnp.arange(owner_count, dtype=jnp.int32)[None, :]).astype(jnp.int32)
    rank = jnp.sum((jnp.cumsum(onehot, axis=0) - onehot) * onehot, axis=1)
    slot = owner * capacity + rank
    request = (
        jnp.zeros((2, owner_count * capacity), jnp.int32)
        .at[:, slot]
        .set(jnp.stack([wanted, viewed]))
    )
    request = request.reshape(2, owner_count, capacity)
    received = lax.all_to_all(request, "tile", split_axis=1, concat_axis=1, tiled=True)
    rows_in = received[0].reshape(-1)
    views_in = received[1].reshape(-1)
    screen = project(params[:, rows_in], cameras[views_in])
    screen = screen.reshape(9, received.shape[1], received.shape[2])
    fetched = lax.all_to_all(screen, "tile", split_axis=1, concat_axis=1, tiled=True)
    entry = fetched.reshape(9, -1)[:, slot].reshape(9, tiles_here, slab).transpose(1, 0, 2)
    order = jnp.arange(slab, dtype=jnp.int32)
    strict = (order[:, None] < order[None, :]).astype(jnp.float32)
    inclusive = (order[:, None] <= order[None, :]).astype(jnp.float32)

    def forward(args):
        screen, alive = args
        offset_x, offset_y, falloff, alpha = coverage(screen, alive, pixels)
        leak = jnp.log1p(-alpha)
        before = running_sum(leak, strict)
        weight = alpha * jnp.exp(before)
        color = jnp.einsum("ck,pk->cp", screen[6:9], weight, precision=highest)
        return (jnp.sum(leak, axis=1), color)

    def backward(args):
        screen, alive, start_log, start_color, whole, miss = args
        offset_x, offset_y, falloff, alpha = coverage(screen, alive, pixels)
        leak = jnp.log1p(-alpha)
        local = running_sum(leak, strict)
        carried = jnp.exp(start_log)[:, None]
        inside = jnp.exp(local)
        trans = carried * inside
        weight = alpha * trans
        local_weight = alpha * inside
        d_alpha = jnp.zeros_like(alpha)
        for channel in range(3):
            shade = screen[6 + channel][None, :]
            upto = running_sum(local_weight * shade, inclusive)
            behind = whole[channel][:, None] - start_color[channel][:, None] - carried * upto
            d_alpha = d_alpha + miss[channel][:, None] * (trans * shade - behind / (1.0 - alpha))
        d_color = jnp.einsum("cp,pk->ck", miss, weight, precision=highest)
        d_quad = d_alpha * (-0.5 * alpha)
        d_opacity = jnp.sum(d_alpha * falloff * alive[None, :], axis=0)
        d_center_x = jnp.sum(
            d_quad * -2.0 * (screen[2][None, :] * offset_x + screen[3][None, :] * offset_y), axis=0
        )
        d_center_y = jnp.sum(
            d_quad * -2.0 * (screen[3][None, :] * offset_x + screen[4][None, :] * offset_y), axis=0
        )
        d_conic_a = jnp.sum(d_quad * offset_x * offset_x, axis=0)
        d_conic_b = jnp.sum(d_quad * 2.0 * offset_x * offset_y, axis=0)
        d_conic_c = jnp.sum(d_quad * offset_y * offset_y, axis=0)
        return jnp.concatenate(
            [
                jnp.stack([d_center_x, d_center_y, d_conic_a, d_conic_b, d_conic_c, d_opacity]),
                d_color,
            ],
            axis=0,
        )

    quarter = tiles_here // depth_count
    whole_entry = lax.all_to_all(entry, "depth", split_axis=0, concat_axis=2, tiled=True)
    first_tile = depth_index * quarter
    own_length = lax.dynamic_slice_in_dim(tile_length, first_tile, quarter, 0)
    full_place = jnp.arange(slab * depth_count, dtype=jnp.int32)
    own_live = (full_place[None, :] < own_length[:, None]).astype(jnp.float32)
    own_log, own_color = lax.map(forward, (whole_entry, own_live))
    own_image = own_color + jnp.exp(own_log)[:, None, :] * background[None, :, None]
    own_error = own_image - lax.dynamic_slice_in_dim(target, first_tile, quarter, 0)
    zero_log = jnp.zeros_like(own_log)
    zero_color = jnp.zeros_like(own_color)
    own_grad = lax.map(
        backward, (whole_entry, own_live, zero_log, zero_color, own_image, own_error)
    )
    entry_grad = lax.all_to_all(own_grad, "depth", split_axis=2, concat_axis=0, tiled=True)
    image = lax.all_gather(own_image, "depth", axis=0, tiled=True)
    flat_grad = entry_grad.transpose(1, 0, 2).reshape(9, -1)
    outgoing = jnp.zeros((9, owner_count * capacity), jnp.float32).at[:, slot].set(flat_grad)
    outgoing = outgoing.reshape(9, owner_count, capacity)
    incoming = lax.all_to_all(outgoing, "tile", split_axis=1, concat_axis=1, tiled=True)
    rows_in = received[0].reshape(-1)
    views_in = received[1].reshape(-1)
    chosen_cams = cameras[views_in]
    unused, pullback = jax.vjp(lambda chosen: project(chosen, chosen_cams), params[:, rows_in])
    (slot_grad,) = pullback(incoming.reshape(9, -1))
    gradient = jnp.zeros_like(params).at[:, rows_in].add(slot_grad)
    gradient = lax.psum(gradient, "depth")
    new_params, new_first, new_second = adam_update(params, first_moment, second_moment, gradient)
    return (image, new_params, new_first, new_second)


def solution(mesh):
    placed = (
        P(None, "tile"),
        P(None, "tile"),
        P(None, "tile"),
        P(None, "tile"),
        P(None, "tile"),
        P(None, "tile"),
        P(),
        P(),
        P("tile", None, None),
        P("tile"),
        P("tile"),
        P("depth", "tile", None, None),
        P("depth", "tile", None),
    )
    return jax.shard_map(
        body,
        mesh=mesh,
        in_specs=placed,
        out_specs=(P("tile", None, None), P(None, "tile"), P(None, "tile"), P(None, "tile")),
        check_vma=False,
    )
```

profile of v0, /device:TPU:0, one launch (start us, length us, event | category | flops | bytes accessed | tf_op | source)
XLA Modules:
  0.0 199.4 jit_solution(7363935695881023951)
XLA Ops:
  7.2 0.7 fusion.58
  7.9 1.1 reduce-window.6
  9.0 0.2 slice_reduce_fusion.2
  9.3 0.8 fusion.55
  10.1 0.7 compare_select_fusion.2
  10.8 0.7 broadcast_in_dim.53
  11.5 0.7 add_bitcast_fusion.1
  12.2 0.1 copy.151
  12.3 1.9 scatter_custom_fusion
  14.2 0.9 copy.152
  15.2 7.3 %all-to-all-start = ((s32[2,8,160]{2,0,1:T(2,128)}), s32[2,8,160]{2,0,1:T(2,128)S(1)}, u32[]{:S(2)}, u32[]{:S(2)}) async-start(s32[2,8,160]{2,0,1:T(2,128)} %copy.152), calls=%async_computation | async-start | bytes 32768 | tf_op jit(solution)/shard_map/all_to_all | solution.py:104
  22.5 0.9 pad_maximum_fusion
  23.4 0.4 copy.154
  23.8 0.6 dynamic_slice.26
  24.3 4.7 %all-to-all-done = s32[2,8,160]{2,0,1:T(2,128)S(1)} async-done(((s32[2,8,160]{2,0,1:T(2,128)}), s32[2,8,160]{2,0,1:T(2,128)S(1)}, u32[]{:S(2)}, u32[]{:S(2)}) %all-to-all-start) | async-done | bytes 10272 | tf_op jit(solution)/shard_map/all_to_all | solution.py:104
  29.2 4.3 %gather_fusion = f32[1280,2,4]{2,1,0:T(2,128)S(1)} fusion(f32[4,2,4]{2,1,0:T(2,128)S(1)} %copy-done.1, s32[2048]{0:T(1024)S(1)} %pad_clamp_fusion.1), kind=kCustom, calls=%fused_computation | custom fusion | bytes 87040 | tf_op jit(solution)/shard_map/gather | solution.py:107
  33.6 1.8 fusion.84
  35.3 36.3 %slice_reduce_fusion = (f32[1280]{0:T(1024)S(1)}, f32[1280]{0:T(1024)S(1)}) fusion(f32[1280,2,4]{2,1,0:T(2,128)S(1)} %gather_fusion), kind=kLoop, calls=%fused_computation.71 | loop fusion | bytes 20480 | tf_op jit(solution)/shard_map/slice | solution.py:15
  71.6 1.3 copy.189
  72.9 0.4 copy.190
  73.4 2.4 %gather_fusion.1 = f32[1280,10]{1,0:T(8,128)S(1)} fusion(f32[10,2048]{0,1:T(8,128)S(1)} %copy.154, s32[2048]{0:T(1024)S(1)} %pad_clamp_fusion), kind=kCustom, calls=%fused_computation.1 | custom fusion | bytes 107520 | tf_op jit(solution)/shard_map/gather | solution.py:107
  75.7 0.2 copy.155
  77.0 0.2 stack.44
  77.3 0.8 reshape.1452
  78.0 3.5 %all-to-all-start.1 = ((f32[8,1,1440]{2,1,0:T(1,128)}), f32[8,1,1440]{2,1,0:T(1,128)S(1)}, u32[]{:S(2)}, u32[]{:S(2)}) async-start(f32[8,1,1440]{2,1,0:T(1,128)} %reshape.1452), calls=%async_computation.1 | async-start | bytes 98304 | tf_op jit(solution)/shard_map/all_to_all | solution.py:109
  81.5 0.7 fusion.74
  82.2 5.9 %all-to-all-done.1 = f32[8,1,1440]{2,1,0:T(1,128)S(1)} async-done(((f32[8,1,1440]{2,1,0:T(1,128)}), f32[8,1,1440]{2,1,0:T(1,128)S(1)}, u32[]{:S(2)}, u32[]{:S(2)}) %all-to-all-start.1) | async-done | bytes 46112 | tf_op jit(solution)/shard_map/all_to_all | solution.py:109
  88.1 0.5 broadcast.1100
  88.6 0.8 reduce.40
  89.5 0.3 copy.164
  89.7 1.0 gather_fusion.2
  90.8 0.7 copy.165
  91.5 3.3 %all-to-all-start.2 = ((f32[4,9,128]{2,1,0:T(8,128)}), f32[4,9,128]{2,1,0:T(8,128)S(1)}, u32[]{:S(2)}, u32[]{:S(2)}) async-start(f32[4,9,128]{2,1,0:T(8,128)} %bitcast.21), calls=%async_computation.2 | async-start | bytes 65536 | tf_op jit(solution)/shard_map/all_to_all | solution.py:161
  94.8 0.7 fusion.75
  95.5 3.2 %all-to-all-done.2 = f32[4,9,128]{2,1,0:T(8,128)S(1)} async-done(((f32[4,9,128]{2,1,0:T(8,128)}), f32[4,9,128]{2,1,0:T(8,128)S(1)}, u32[]{:S(2)}, u32[]{:S(2)}) %all-to-all-start.2) | async-done | bytes 18464 | tf_op jit(solution)/shard_map/all_to_all | solution.py:161
  98.7 2.0 fusion.28
  100.8 5.9 %multiply_reduce_fusion.3 = (f32[1024,4]{0,1:T(4,128)S(1)}, f32[1024,4]{0,1:T(4,128)S(1)}, f32[1024,4]{0,1:T(4,128)S(1)}, f32[1024,4,128]{0,2,1:T(8,128)S(1)}, f32[1024,4,128]{0,2,1:T(8,128)}) fusion(f32[4,128]{1,0:T(4,128)S(1)} %bitcast.208, f32[4,128]{1,0:T(4,128)S(1)} %bitcast.188, f32[4,128]{1,0:T(4,128)S(1)} %bitcast.185, f32[1024,4]{0,1:T(4,128)S(1)} %sub.316, ...), kind=kOutput, calls=%fused_computation.60 | convolution fusion | flops 823660544 | bytes 4288512 | tf_op jit(solution)/shard_map/while/body/eval_jaxpr/pbk,kj->pbj/dot_general | solution.py:55
  106.7 2.9 %fusion.24 = f32[1024,4,128]{0,2,1:T(8,128)} fusion(f32[1024,4,128]{0,2,1:T(8,128)S(1)} %get-tuple-element.96, f32[4,128]{1,0:T(4,128)S(1)} %bitcast.189), kind=kOutput, calls=%fused_computation.58 | convolution fusion | flops 805847040 | bytes 4196352 | tf_op jit(solution)/shard_map/while/body/eval_jaxpr/pbk,kj->pbj/dot_general | solution.py:55
  109.6 2.9 %fusion.22 = f32[1024,4,128]{0,2,1:T(8,128)} fusion(f32[1024,4,128]{0,2,1:T(8,128)S(1)} %get-tuple-element.96, f32[4,128]{1,0:T(4,128)S(1)} %bitcast.186), kind=kOutput, calls=%fused_computation.55 | convolution fusion | flops 805847040 | bytes 4196352 | tf_op jit(solution)/shard_map/while/body/eval_jaxpr/pbk,kj->pbj/dot_general | solution.py:55
  112.5 1.9 fusion.14
  114.4 1.1 copy_subtract_fusion
  115.5 1.8 fusion.56
  117.5 6.2 %multiply_multiply_fusion = (f32[1024,4,128]{0,2,1:T(8,128)S(1)}, f32[1024,4,128]{0,2,1:T(8,128)S(1)}) fusion(f32[4,128]{1,0:T(4,128)S(1)} %fusion.74, f32[4,128]{1,0:T(4,128)S(1)} %bitcast.168, f32[4,128]{1,0:T(4,128)S(1)} %bitcast.173, f32[1024]{0:T(1024)S(1)} %get-tuple-element.136, f32[4,128]{1,0:T(4,128)S(1)} %broadcast_multiply_fusion.1, ...), kind=kOutput, calls=%fused_computation.49 | convolution fusion | flops 825245696 | bytes 12701696 | tf_op jit(solution)/shard_map/while/body/eval_jaxpr/pbk,kj->pbj/dot_general | solution.py:55
  123.7 3.8 %fusion.3 = (f32[4,128]{1,0:T(4,128)S(1)}, f32[4,128]{1,0:T(4,128)S(1)}, f32[4,128]{1,0:T(4,128)S(1)}, f32[4,128]{1,0:T(4,128)S(1)}, f32[4,128]{1,0:T(4,128)S(1)}, /*index=5*/f32[4,128]{1,0:T(4,128)S(1)}) fusion(f32[1024,4,128]{0,2,1:T(8,128)S(1)} %get-tuple-element.131, f32[4,128]{1,0:T(4,128)S(1)} %bitcast.162, f32[4,128]{1,0:T(4,128)S(1)} %bitcast.169, ...), kind=kLoop, calls=%fused_computation.29 | loop fusion | flops 17298432 | bytes 4229120 | tf_op jit(solution)/shard_map/while/body/eval_jaxpr/reduce_sum | solution.py:146
  127.7 0.1 copy.174
  127.9 1.3 reduce.41
  129.2 0.2 reshape.1454
  129.4 6.2 %all_to_all.48 = f32[4,1,1152]{2,1,0:T(1,128)S(1)} all-to-all(f32[4,1,1152]{2,1,0:T(1,128)S(1)} %reshape.1454), channel_id=1, replica_groups=mesh['tile'=8,'depth'=4] {'depth'}, dimensions={0} | all-to-all | bytes 36864 | tf_op jit(solution)/shard_map/all_to_all | solution.py:174
  135.6 0.7 reduce.42
  136.3 0.4 reshape.1455
  136.8 0.2 copy.188
  137.0 1.9 scatter_custom_fusion.1
  138.9 0.3 copy.177
  139.2 0.1 reshape.1456
  139.3 9.2 %all_to_all.49 = f32[8,1,1440]{2,1,0:T(1,128)S(1)} all-to-all(f32[8,1,1440]{2,1,0:T(1,128)S(1)} %reshape.1456), channel_id=1, replica_groups=mesh['tile'=8,'depth'=4] {'tile'}, dimensions={0} | all-to-all | bytes 92160 | tf_op jit(solution)/shard_map/all_to_all | solution.py:179
  148.5 0.8 reduce.43
  149.5 0.2 slice_reduce_fusion.11
  150.5 0.3 copy.178
  150.8 9.2 %scatter_custom_fusion.2 = f32[10,2048]{0,1:T(8,128)S(1)} fusion(s32[1280]{0:T(1024)S(1)} %fusion.60, f32[1280,10]{1,0:T(8,128)S(1)} %copy.178, f32[]{:T(128)} %constant.132.clone.1), kind=kCustom, calls=%fused_computation.73 | custom fusion | flops 12800 | bytes 81924 | tf_op jit(solution)/shard_map/scatter-add | solution.py:185
  160.0 1.0 copy.179
  161.0 5.2 %all-gather.1 = f32[4,3,1024]{2,1,0:T(4,128)S(1)} all-gather(f32[1,3,1024]{2,1,0:T(4,128)S(1)} %get-tuple-element.130), channel_id=2, replica_groups=mesh['tile'=8,'depth'=4] {'depth'}, dimensions={0}, use_global_device_ids=true | all-gather | bytes 61440 | tf_op jit(solution)/shard_map/all_gather | solution.py:175
  166.2 0.7 copy.180
  166.8 23.9 %all-reduce.8.cloned.1.call-done = f32[10,2048]{1,0:T(8,128)} async-done(((f32[10,2048]{1,0:T(8,128)}), f32[10,2048]{1,0:T(8,128)}) %all-reduce.8.cloned.1.call-update) | async-done | bytes 81936 | tf_op jit(solution)/shard_map/psum | solution.py:186
  190.8 1.7 multiply_subtract_fusion
  (87 shorter events, 3.0 us)
Async XLA Ops:
  7.2 15.3 %copy-start = (f32[4,3,1024]{2,0,1:T(4,128)S(1)}, f32[4,3,1024]{2,0,1:T(4,128)}, u32[]{:S(2)}) copy-start(f32[4,3,1024]{2,0,1:T(4,128)} %param.21) | copy-start | bytes 147460
  7.2 16.6 %copy-start.9 = (s32[4]{0:T(128)S(1)}, s32[4]{0:T(128)}, u32[]{:S(2)}) copy-start(s32[4]{0:T(128)} %param.23) | copy-start | bytes 52
  7.2 22.0 %copy-start.1 = (f32[4,2,4]{2,1,0:T(2,128)S(1)}, f32[4,2,4]{2,1,0:T(2,128)}, u32[]{:S(2)}) copy-start(f32[4,2,4]{2,1,0:T(2,128)} %param.19) | copy-start | bytes 388
  15.2 13.9 %all-to-all-start = ((s32[2,8,160]{2,0,1:T(2,128)}), s32[2,8,160]{2,0,1:T(2,128)S(1)}, u32[]{:S(2)}, u32[]{:S(2)}) async-start(s32[2,8,160]{2,0,1:T(2,128)} %copy.152), calls=%async_computation | async-start | bytes 32768 | tf_op jit(solution)/shard_map/all_to_all | solution.py:104
  78.0 10.1 %all-to-all-start.1 = ((f32[8,1,1440]{2,1,0:T(1,128)}), f32[8,1,1440]{2,1,0:T(1,128)S(1)}, u32[]{:S(2)}, u32[]{:S(2)}) async-start(f32[8,1,1440]{2,1,0:T(1,128)} %reshape.1452), calls=%async_computation.1 | async-start | bytes 98304 | tf_op jit(solution)/shard_map/all_to_all | solution.py:109
  91.5 7.2 %all-to-all-start.2 = ((f32[4,9,128]{2,1,0:T(8,128)}), f32[4,9,128]{2,1,0:T(8,128)S(1)}, u32[]{:S(2)}, u32[]{:S(2)}) async-start(f32[4,9,128]{2,1,0:T(8,128)} %bitcast.21), calls=%async_computation.2 | async-start | bytes 65536 | tf_op jit(solution)/shard_map/all_to_all | solution.py:161
  94.8 96.0 %all-reduce.8.cloned.1.call-start = ((), (), s32[]{:S(2)}) async-start(), calls=%async_computation.5 | async-start | bytes 262144 | tf_op jit(solution)/shard_map/psum | solution.py:186
  109.6 4.8 %copy-start.8 = (f32[3]{0:T(128)S(1)}, f32[3]{0:T(128)}, u32[]{:S(2)}) copy-start(f32[3]{0:T(128)} %param.20) | copy-start | bytes 40
  149.3 41.5 %copy-start.2 = (f32[3,2048]{1,0:T(4,128)S(1)}, f32[3,2048]{1,0:T(4,128)}, u32[]{:S(2)}) copy-start(f32[3,2048]{1,0:T(4,128)} %param.16) | copy-start | bytes 73732
  149.3 41.5 %copy-start.3 = (f32[3,2048]{1,0:T(4,128)S(1)}, f32[3,2048]{1,0:T(4,128)}, u32[]{:S(2)}) copy-start(f32[3,2048]{1,0:T(4,128)} %param.14) | copy-start | bytes 73732
  149.3 41.4 %copy-start.4 = (f32[3,2048]{1,0:T(4,128)S(1)}, f32[3,2048]{1,0:T(4,128)}, u32[]{:S(2)}) copy-start(f32[3,2048]{1,0:T(4,128)} %param.13) | copy-start | bytes 73732
  149.3 41.4 %copy-start.5 = (f32[10,2048]{1,0:T(8,128)S(1)}, f32[10,2048]{1,0:T(8,128)}, u32[]{:S(2)}) copy-start(f32[10,2048]{1,0:T(8,128)} %param.17) | copy-start | bytes 245764
  149.3 41.4 %copy-start.6 = (f32[10,2048]{1,0:T(8,128)S(1)}, f32[10,2048]{1,0:T(8,128)}, u32[]{:S(2)}) copy-start(f32[10,2048]{1,0:T(8,128)} %param.18) | copy-start | bytes 245764
  149.3 41.4 %copy-start.7 = (f32[1,2048]{1,0:T(1,128)S(1)}, f32[1,2048]{1,0:T(1,128)}, u32[]{:S(2)}) copy-start(f32[1,2048]{1,0:T(1,128)} %param.15) | copy-start | bytes 24580
Sparse Core Ops, SparseCore 0:
  161.1 29.6 all-reduce.7
where the time goes:
time: 200 us; the launch traced here: 199 us
  local copies, waits for them, and re-layouts  62.6 us (31%)
  waiting for transfers between devices  37.7 us (19%)
  other arithmetic  29 us (14%)
  matrix products  20.8 us (10%)
  blocking collectives  20.6 us (10%)
  between operations  14.6 us (7%)
  starting transfers between devices  14.1 us (7%)
    slice x1, local copies, waits for them, and re-layouts, project(): cams[:, 1, 3]  36.3 us
    psum x1, waiting for transfers between devices, body(): gradient = lax.psum(gradient, 'depth')  23.9 us
    dot_general x4, matrix products, running_sum(): jnp.einsum('pbk,kj->pbj', blocks, triangle, precision=lax.Precision.HIGHEST)  17.8 us
    scatter-add x1, other arithmetic, body(): gradient = jnp.zeros_like(params).at[:, rows_in].add(slot_grad)  9.18 us
    all_to_all x1, blocking collectives, body(): lax.all_to_all(outgoing, 'tile', split_axis=1, concat_axis=1, tiled=True)  9.17 us
    all_to_all x1, starting transfers between devices, body(): lax.all_to_all(request, 'tile', split_axis=1, concat_axis=1, tiled=True)  7.31 us
    gather x3, local copies, waits for them, and re-layouts, body(): screen = project(params[:, rows_in], cameras[views_in])  6.92 us
    all_to_all x1, blocking collectives, body(): lax.all_to_all(own_grad, 'depth', split_axis=2, concat_axis=0, tiled=True)  6.22 us
  transfers between devices with their start and end apart: 4, of which 4 were waited for; matrix products, arithmetic and copies ran while one was open for 2% of the time, Pallas kernels for 0%

commit v1 on v0

--- a/solution.py
+++ b/solution.py
@@ -183,7 +183,11 @@
     unused, pullback = jax.vjp(lambda chosen: project(chosen, chosen_cams), params[:, rows_in])
     (slot_grad,) = pullback(incoming.reshape(9, -1))
     gradient = jnp.zeros_like(params).at[:, rows_in].add(slot_grad)
-    gradient = lax.psum(gradient, "depth")
+    gradient = gradient
+    for hop in (1, 2):
+        gradient = gradient + lax.ppermute(
+            gradient, "depth", [(dev, dev ^ hop) for dev in range(4)]
+        )
     new_params, new_first, new_second = adam_update(params, first_moment, second_moment, gradient)
     return (image, new_params, new_first, new_second)
 

time: 200 us -> 165 us (0.82)
  waiting for transfers between devices: 37.7 us -> 15.2 us
  between operations: 14.6 us -> 1.23 us
    psum x1 -> x0, waiting for transfers between devices: 23.9 us -> none  [body(): gradient = lax.psum(gradient, 'depth')]
  transfers between devices with their start and end apart: 4 -> 5, of which waited for: 4 -> 4; matrix products, arithmetic and copies ran while one was open for 2% -> 2% of each run, Pallas kernels for 0% -> 0%
where the time goes in v1:
time: 165 us; the launch traced here: 164 us
  local copies, waits for them, and re-layouts  61.9 us (38%)
  other arithmetic  28.4 us (17%)
  blocking collectives  22.1 us (13%)
  matrix products  20.9 us (13%)
  waiting for transfers between devices  15.2 us (9%)
  starting transfers between devices  14.2 us (9%)
    slice x1, local copies, waits for them, and re-layouts, project(): cams[:, 1, 3]  36.3 us
    dot_general x4, matrix products, running_sum(): jnp.einsum('pbk,kj->pbj', blocks, triangle, precision=lax.Precision.HIGHEST)  17.9 us
    scatter-add x1, other arithmetic, body(): gradient = jnp.zeros_like(params).at[:, rows_in].add(slot_grad)  9.18 us
    all_to_all x1, blocking collectives, body(): lax.all_to_all(outgoing, 'tile', split_axis=1, concat_axis=1, tiled=True)  9.17 us
    all_to_all x1, starting transfers between devices, body(): lax.all_to_all(request, 'tile', split_axis=1, concat_axis=1, tiled=True)  7.31 us
    gather x3, local copies, waits for them, and re-layouts, body(): screen = project(params[:, rows_in], cameras[views_in])  6.92 us
    all_gather x1, blocking collectives, body(): image = lax.all_gather(own_image, 'depth', axis=0, tiled=True)  6.7 us
    all_to_all x1, blocking collectives, body(): lax.all_to_all(own_grad, 'depth', split_axis=2, concat_axis=0, tiled=True)  6.22 us
  transfers between devices with their start and end apart: 5, of which 4 were waited for; matrix products, arithmetic and copies ran while one was open for 2% of the time, Pallas kernels for 0%

profile of v1, /device:TPU:0, one launch (start us, length us, event | category | flops | bytes accessed | tf_op | source)
XLA Modules:
  0.0 163.9 jit_solution(12470973169211693344)
XLA Ops:
  0.7 0.7 fusion.58
  1.4 1.1 reduce-window.6
  2.5 0.2 slice_reduce_fusion.2
  2.8 0.8 fusion.55
  3.5 0.7 compare_select_fusion.2
  4.2 0.7 broadcast_in_dim.53
  5.0 0.7 add_bitcast_fusion.1
  5.6 0.1 copy.159
  5.8 1.9 %scatter_custom_fusion = s32[2,1280]{0,1:T(8,128)S(1)} fusion(s32[512]{0:T(512)S(1)} %bitcast.197, s32[512,2]{1,0:T(8,128)S(1)} %copy.159, s32[]{:T(128)} %constant.127.clone.1), kind=kCustom, calls=%fused_computation.77 | custom fusion | bytes 10244 | tf_op jit(solution)/shard_map/scatter | solution.py:101
  7.7 0.9 copy.160
  8.6 7.3 %all-to-all-start = ((s32[2,8,160]{2,0,1:T(2,128)}), s32[2,8,160]{2,0,1:T(2,128)S(1)}, u32[]{:S(2)}, u32[]{:S(2)}) async-start(s32[2,8,160]{2,0,1:T(2,128)} %copy.160), calls=%async_computation | async-start | bytes 32768 | tf_op jit(solution)/shard_map/all_to_all | solution.py:104
  16.0 0.9 pad_maximum_fusion
  16.8 0.4 copy.162
  17.2 0.6 dynamic_slice.26
  17.8 4.7 %all-to-all-done = s32[2,8,160]{2,0,1:T(2,128)S(1)} async-done(((s32[2,8,160]{2,0,1:T(2,128)}), s32[2,8,160]{2,0,1:T(2,128)S(1)}, u32[]{:S(2)}, u32[]{:S(2)}) %all-to-all-start) | async-done | bytes 10272 | tf_op jit(solution)/shard_map/all_to_all | solution.py:104
  22.7 4.3 %gather_fusion = f32[1280,2,4]{2,1,0:T(2,128)S(1)} fusion(f32[4,2,4]{2,1,0:T(2,128)S(1)} %copy-done.1, s32[2048]{0:T(1024)S(1)} %pad_clamp_fusion.1), kind=kCustom, calls=%fused_computation | custom fusion | bytes 87040 | tf_op jit(solution)/shard_map/gather | solution.py:107
  27.0 1.8 %fusion.84 = (f32[1280,1,3]{2,1,0:T(1,128)S(1)}, f32[1280,1,3]{2,1,0:T(1,128)}) fusion(f32[1280,2,4]{2,1,0:T(2,128)S(1)} %gather_fusion), kind=kLoop, calls=%fused_computation.179 | loop fusion | bytes 61440 | tf_op jit(solution)/shard_map/slice | solution.py:13
  28.8 36.3 %slice_reduce_fusion = (f32[1280]{0:T(1024)S(1)}, f32[1280]{0:T(1024)S(1)}) fusion(f32[1280,2,4]{2,1,0:T(2,128)S(1)} %gather_fusion), kind=kLoop, calls=%fused_computation.71 | loop fusion | bytes 20480 | tf_op jit(solution)/shard_map/slice | solution.py:15
  65.1 1.3 copy.198
  66.3 0.4 copy.199
  66.8 2.4 %gather_fusion.1 = f32[1280,10]{1,0:T(8,128)S(1)} fusion(f32[10,2048]{0,1:T(8,128)S(1)} %copy.162, s32[2048]{0:T(1024)S(1)} %pad_clamp_fusion), kind=kCustom, calls=%fused_computation.1 | custom fusion | bytes 107520 | tf_op jit(solution)/shard_map/gather | solution.py:107
  69.2 0.2 copy.163
  70.5 0.2 stack.44
  70.7 0.8 reshape.1452
  71.5 3.5 %all-to-all-start.1 = ((f32[8,1,1440]{2,1,0:T(1,128)}), f32[8,1,1440]{2,1,0:T(1,128)S(1)}, u32[]{:S(2)}, u32[]{:S(2)}) async-start(f32[8,1,1440]{2,1,0:T(1,128)} %reshape.1452), calls=%async_computation.1 | async-start | bytes 98304 | tf_op jit(solution)/shard_map/all_to_all | solution.py:109
  75.0 0.7 fusion.74
  75.7 5.9 %all-to-all-done.1 = f32[8,1,1440]{2,1,0:T(1,128)S(1)} async-done(((f32[8,1,1440]{2,1,0:T(1,128)}), f32[8,1,1440]{2,1,0:T(1,128)S(1)}, u32[]{:S(2)}, u32[]{:S(2)}) %all-to-all-start.1) | async-done | bytes 46112 | tf_op jit(solution)/shard_map/all_to_all | solution.py:109
  81.6 0.5 broadcast.1100
  82.1 0.8 reduce.40
  82.9 0.3 copy.172
  83.2 1.0 gather_fusion.2
  84.2 0.7 copy.173
  85.0 3.3 %all-to-all-start.2 = ((f32[4,9,128]{2,1,0:T(8,128)}), f32[4,9,128]{2,1,0:T(8,128)S(1)}, u32[]{:S(2)}, u32[]{:S(2)}) async-start(f32[4,9,128]{2,1,0:T(8,128)} %bitcast.21), calls=%async_computation.2 | async-start | bytes 65536 | tf_op jit(solution)/shard_map/all_to_all | solution.py:161
  88.3 0.7 fusion.75
  88.9 3.3 %all-to-all-done.2 = f32[4,9,128]{2,1,0:T(8,128)S(1)} async-done(((f32[4,9,128]{2,1,0:T(8,128)}), f32[4,9,128]{2,1,0:T(8,128)S(1)}, u32[]{:S(2)}, u32[]{:S(2)}) %all-to-all-start.2) | async-done | bytes 18464 | tf_op jit(solution)/shard_map/all_to_all | solution.py:161
  92.2 2.0 %fusion.28 = f32[1024,4]{0,1:T(4,128)S(1)} fusion(f32[4,128]{1,0:T(4,128)S(1)} %fusion.74, f32[4,128]{1,0:T(4,128)S(1)} %bitcast.165, f32[4,128]{1,0:T(4,128)S(1)} %bitcast.170, f32[1024]{0:T(1024)S(1)} %get-tuple-element.136, f32[4,128]{1,0:T(4,128)S(1)} %broadcast_multiply_fusion.1, f32[4,128]{1,0:T(4,128)S(1)} %bitcast.175, ...), kind=kLoop, calls=%fused_computation.63 | loop fusion | flops 7860224 | bytes 38912 | tf_op jit(solution)/shard_map/while/body/eval_jaxpr/reduce_sum | solution.py:56
  94.2 5.9 %multiply_reduce_fusion.3 = (f32[1024,4]{0,1:T(4,128)S(1)}, f32[1024,4]{0,1:T(4,128)S(1)}, f32[1024,4]{0,1:T(4,128)S(1)}, f32[1024,4,128]{0,2,1:T(8,128)S(1)}, f32[1024,4,128]{0,2,1:T(8,128)}) fusion(f32[4,128]{1,0:T(4,128)S(1)} %bitcast.208, f32[4,128]{1,0:T(4,128)S(1)} %bitcast.188, f32[4,128]{1,0:T(4,128)S(1)} %bitcast.185, f32[1024,4]{0,1:T(4,128)S(1)} %sub.316, ...), kind=kOutput, calls=%fused_computation.60 | convolution fusion | flops 823660544 | bytes 4288512 | tf_op jit(solution)/shard_map/while/body/eval_jaxpr/pbk,kj->pbj/dot_general | solution.py:55
  100.1 2.9 %fusion.24 = f32[1024,4,128]{0,2,1:T(8,128)} fusion(f32[1024,4,128]{0,2,1:T(8,128)S(1)} %get-tuple-element.96, f32[4,128]{1,0:T(4,128)S(1)} %bitcast.189), kind=kOutput, calls=%fused_computation.58 | convolution fusion | flops 805847040 | bytes 4196352 | tf_op jit(solution)/shard_map/while/body/eval_jaxpr/pbk,kj->pbj/dot_general | solution.py:55
  103.0 2.9 %fusion.22 = f32[1024,4,128]{0,2,1:T(8,128)} fusion(f32[1024,4,128]{0,2,1:T(8,128)S(1)} %get-tuple-element.96, f32[4,128]{1,0:T(4,128)S(1)} %bitcast.186), kind=kOutput, calls=%fused_computation.55 | convolution fusion | flops 805847040 | bytes 4196352 | tf_op jit(solution)/shard_map/while/body/eval_jaxpr/pbk,kj->pbj/dot_general | solution.py:55
  105.9 1.9 %fusion.14 = f32[1024]{0:T(1024)S(1)} fusion(f32[512]{0:T(512)S(1)} %fusion.75, f32[512]{0:T(512)S(1)} %bitcast.167, f32[512]{0:T(512)S(1)} %bitcast.172, f32[1024]{0:T(1024)S(1)} %get-tuple-element.136, f32[512]{0:T(512)S(1)} %bitcast.214, f32[512]{0:T(512)S(1)} %bitcast.177, f32[1024]{0:T(1024)S(1)} %get-tuple-element.135, f32[512]{0:T(512)S(1)} %bitcast.182, ...), kind=kLoop, calls=%fused_computation.40 | loop fusion | flops 7863296 | bytes 26624 | tf_op jit(solution)/shard_map/while/body/eval_jaxpr/reduce_sum | solution.py:122
  107.8 1.1 copy_subtract_fusion
  108.9 1.8 %fusion.56 = f32[3,512]{1,0:T(4,128)S(1)} fusion(f32[1024,512]{0,1:T(8,128)S(1)} %bitcast.142, f32[1,3,1024]{2,1,0:T(4,128)S(1)} %get-tuple-element.129), kind=kOutput, calls=%fused_computation.112 | convolution fusion | flops 18874368 | bytes 2115584 | tf_op jit(solution)/shard_map/while/body/eval_jaxpr/cp,pk->ck/dot_general | solution.py:140
  111.0 6.3 %multiply_multiply_fusion = (f32[1024,4,128]{0,2,1:T(8,128)S(1)}, f32[1024,4,128]{0,2,1:T(8,128)S(1)}) fusion(f32[4,128]{1,0:T(4,128)S(1)} %fusion.74, f32[4,128]{1,0:T(4,128)S(1)} %bitcast.168, f32[4,128]{1,0:T(4,128)S(1)} %bitcast.173, f32[1024]{0:T(1024)S(1)} %get-tuple-element.136, f32[4,128]{1,0:T(4,128)S(1)} %broadcast_multiply_fusion.1, ...), kind=kOutput, calls=%fused_computation.49 | convolution fusion | flops 825245696 | bytes 12701696 | tf_op jit(solution)/shard_map/while/body/eval_jaxpr/pbk,kj->pbj/dot_general | solution.py:55
  117.3 4.1 %fusion.3 = (f32[4,128]{1,0:T(4,128)S(1)}, f32[4,128]{1,0:T(4,128)S(1)}, f32[4,128]{1,0:T(4,128)S(1)}, f32[4,128]{1,0:T(4,128)S(1)}, f32[4,128]{1,0:T(4,128)S(1)}, /*index=5*/f32[4,128]{1,0:T(4,128)S(1)}) fusion(f32[1024,4,128]{0,2,1:T(8,128)S(1)} %get-tuple-element.131, f32[4,128]{1,0:T(4,128)S(1)} %bitcast.162, f32[4,128]{1,0:T(4,128)S(1)} %bitcast.169, ...), kind=kLoop, calls=%fused_computation.29 | loop fusion | flops 17298432 | bytes 4229120 | tf_op jit(solution)/shard_map/while/body/eval_jaxpr/reduce_sum | solution.py:146
  121.6 0.1 copy.182
  121.7 1.3 reduce.41
  123.0 0.2 reshape.1454
  123.2 6.2 %all_to_all.48 = f32[4,1,1152]{2,1,0:T(1,128)S(1)} all-to-all(f32[4,1,1152]{2,1,0:T(1,128)S(1)} %reshape.1454), channel_id=1, replica_groups=mesh['tile'=8,'depth'=4] {'depth'}, dimensions={0} | all-to-all | bytes 36864 | tf_op jit(solution)/shard_map/all_to_all | solution.py:174
  129.5 0.7 reduce.42
  130.2 0.4 reshape.1455
  130.7 0.2 copy.197
  130.8 1.9 %scatter_custom_fusion.1 = f32[9,1280]{0,1:T(8,128)S(1)} fusion(s32[512]{0:T(512)S(1)} %bitcast.199, f32[512,9]{1,0:T(8,128)S(1)} %bitcast.156, f32[]{:T(128)} %constant.132.clone.1), kind=kCustom, calls=%fused_computation.75 | custom fusion | bytes 46084 | tf_op jit(solution)/shard_map/scatter | solution.py:177
  132.7 0.3 copy.185
  133.1 0.1 reshape.1456
  133.2 9.2 %all_to_all.49 = f32[8,1,1440]{2,1,0:T(1,128)S(1)} all-to-all(f32[8,1,1440]{2,1,0:T(1,128)S(1)} %reshape.1456), channel_id=1, replica_groups=mesh['tile'=8,'depth'=4] {'tile'}, dimensions={0} | all-to-all | bytes 92160 | tf_op jit(solution)/shard_map/all_to_all | solution.py:179
  142.4 0.8 reduce.43
  143.3 0.2 slice_reduce_fusion.11
  144.4 0.3 copy.186
  144.6 9.2 %scatter_custom_fusion.2 = f32[10,2048]{0,1:T(8,128)S(1)} fusion(s32[1280]{0:T(1024)S(1)} %fusion.60, f32[1280,10]{1,0:T(8,128)S(1)} %copy.186, f32[]{:T(128)} %constant.132.clone.1), kind=kCustom, calls=%fused_computation.73 | custom fusion | flops 12800 | bytes 81924 | tf_op jit(solution)/shard_map/scatter-add | solution.py:185
  153.8 0.3 copy.188
  154.2 1.3 collective-permute-done
  155.6 6.7 %all-gather.1 = f32[4,3,1024]{2,1,0:T(4,128)S(1)} all-gather(f32[1,3,1024]{2,1,0:T(4,128)S(1)} %get-tuple-element.130), channel_id=2, replica_groups=mesh['tile'=8,'depth'=4] {'depth'}, dimensions={0}, use_global_device_ids=true | all-gather | bytes 61440 | tf_op jit(solution)/shard_map/all_gather | solution.py:175
  162.3 0.7 copy.189
  163.0 0.8 multiply_subtract_fusion
  (89 shorter events, 3.1 us)
Async XLA Ops:
  0.6 15.3 %copy-start = (f32[4,3,1024]{2,0,1:T(4,128)S(1)}, f32[4,3,1024]{2,0,1:T(4,128)}, u32[]{:S(2)}) copy-start(f32[4,3,1024]{2,0,1:T(4,128)} %param.21) | copy-start | bytes 147460
  0.6 16.6 %copy-start.9 = (s32[4]{0:T(128)S(1)}, s32[4]{0:T(128)}, u32[]{:S(2)}) copy-start(s32[4]{0:T(128)} %param.23) | copy-start | bytes 52
  0.7 22.0 %copy-start.1 = (f32[4,2,4]{2,1,0:T(2,128)S(1)}, f32[4,2,4]{2,1,0:T(2,128)}, u32[]{:S(2)}) copy-start(f32[4,2,4]{2,1,0:T(2,128)} %param.19) | copy-start | bytes 388
  8.6 13.9 %all-to-all-start = ((s32[2,8,160]{2,0,1:T(2,128)}), s32[2,8,160]{2,0,1:T(2,128)S(1)}, u32[]{:S(2)}, u32[]{:S(2)}) async-start(s32[2,8,160]{2,0,1:T(2,128)} %copy.160), calls=%async_computation | async-start | bytes 32768 | tf_op jit(solution)/shard_map/all_to_all | solution.py:104
  71.5 10.1 %all-to-all-start.1 = ((f32[8,1,1440]{2,1,0:T(1,128)}), f32[8,1,1440]{2,1,0:T(1,128)S(1)}, u32[]{:S(2)}, u32[]{:S(2)}) async-start(f32[8,1,1440]{2,1,0:T(1,128)} %reshape.1452), calls=%async_computation.1 | async-start | bytes 98304 | tf_op jit(solution)/shard_map/all_to_all | solution.py:109
  85.0 7.2 %all-to-all-start.2 = ((f32[4,9,128]{2,1,0:T(8,128)}), f32[4,9,128]{2,1,0:T(8,128)S(1)}, u32[]{:S(2)}, u32[]{:S(2)}) async-start(f32[4,9,128]{2,1,0:T(8,128)} %bitcast.21), calls=%async_computation.2 | async-start | bytes 65536 | tf_op jit(solution)/shard_map/all_to_all | solution.py:161
  103.0 4.8 %copy-start.8 = (f32[3]{0:T(128)S(1)}, f32[3]{0:T(128)}, u32[]{:S(2)}) copy-start(f32[3]{0:T(128)} %param.20) | copy-start | bytes 40
  143.2 19.8 %copy-start.2 = (f32[3,2048]{1,0:T(4,128)S(1)}, f32[3,2048]{1,0:T(4,128)}, u32[]{:S(2)}) copy-start(f32[3,2048]{1,0:T(4,128)} %param.16) | copy-start | bytes 73732
  143.3 19.7 %copy-start.3 = (f32[3,2048]{1,0:T(4,128)S(1)}, f32[3,2048]{1,0:T(4,128)}, u32[]{:S(2)}) copy-start(f32[3,2048]{1,0:T(4,128)} %param.14) | copy-start | bytes 73732
  143.3 19.7 %copy-start.4 = (f32[3,2048]{1,0:T(4,128)S(1)}, f32[3,2048]{1,0:T(4,128)}, u32[]{:S(2)}) copy-start(f32[3,2048]{1,0:T(4,128)} %param.13) | copy-start | bytes 73732
  143.3 19.7 %copy-start.5 = (f32[10,2048]{1,0:T(8,128)S(1)}, f32[10,2048]{1,0:T(8,128)}, u32[]{:S(2)}) copy-start(f32[10,2048]{1,0:T(8,128)} %param.17) | copy-start | bytes 245764
  143.3 19.7 %copy-start.6 = (f32[10,2048]{1,0:T(8,128)S(1)}, f32[10,2048]{1,0:T(8,128)}, u32[]{:S(2)}) copy-start(f32[10,2048]{1,0:T(8,128)} %param.18) | copy-start | bytes 245764
  143.3 19.7 %copy-start.7 = (f32[1,2048]{1,0:T(1,128)S(1)}, f32[1,2048]{1,0:T(1,128)}, u32[]{:S(2)}) copy-start(f32[1,2048]{1,0:T(1,128)} %param.15) | copy-start | bytes 24580
  154.1 1.4 collective-permute-start
  155.5 7.4 %collective-permute-start.1 = (f32[10,2048]{1,0:T(8,128)S(1)}, f32[10,2048]{1,0:T(8,128)S(1)}, u32[]{:S(2)}, u32[]{:S(2)}) collective-permute-start(f32[10,2048]{1,0:T(8,128)S(1)} %add.398), channel_id=1, source_target_pairs={{0,2},{1,3},{2,0},{3,1},{4,6},{5,7},{6,4},{7,5},{8,10},{9,11},{10,... | collective-permute-start | bytes 245768 | tf_op jit(solution)/shard_map/ppermute | solution.py:188
